TPU v7x, 256 devices: a whole 4x4x8 slice. The times are simulated.
256 devices in a mesh: fsdp: 16 (over z, x_lo), tp: 8 (over y, core), rep: 2 (over x_hi).
Axes of the slice: x: 4 (x_hi: 2, x_lo: 2; x = x_hi * 2 + x_lo), y: 4, z: 8, core: 2. Of those that a mesh axis runs over, the one named last changes fastest.
Arguments:
- hidden: bfloat16 [4096, 16384], P(('rep', 'fsdp')), parts along dimension 0, may hold values from -400 to 400
- base_weight: bfloat16 [32768, 16384], P(('rep', 'fsdp', 'tp')), parts along dimension 0, may hold values from -1 to 1
- adapter_down: bfloat16 [32768, 32], P(('rep', 'fsdp', 'tp')), parts along dimension 0, may hold values from -0.046875 to 0.046875
- adapter_up: bfloat16 [64, 16384], P('rep'), parts along dimension 0, may hold values from -0.1796875 to 0.1796875
- norm_gain: bfloat16 [32768], P('rep'), parts along dimension 0, may hold values from 0.25 to 1.75
- positions: int32 [4096], P(('rep', 'fsdp')), parts along dimension 0, may hold values from 0 to 6142, as said below
Outputs:
- queries: bfloat16 [4096, 16384], P(('rep', 'fsdp'), 'tp'), parts along dimension 0
There are 2 independent parts, one for each index of `rep`. A program takes and returns all parts, laid end to end along the dimension named above; each array names one. Nothing has to cross between parts.
Inputs may be any that keep to these rules, and one draw needn't show every extreme that they name: Within a document positions rise by one from token to token; every document after the first starts at 0; the first document continues an earlier one and its last token has position 6142.
All inputs are finite; a program needn't handle non-finite values.
Results may differ from a plain program's by a relative error of at most 0.018.
Values may be sent and summed in bfloat16 or wider, within the bound.
A program may use at most 128 MiB of HBM per device.

v0:
```python
import math

import jax
import jax.numpy as jnp
from jax import lax
from jax.sharding import PartitionSpec as P

HEAD = 128
BLOCK = 128


norm_epsilon = 1e-05
scale_epsilon = 1e-06
code_limit = 15.0
adapter_scale = 2.0
rope_theta = 500000.0
rope_factor = 8.0
low_factor = 1.0
high_factor = 4.0
initial_context = 8192.0


def normalize(hidden, norm_gain):
    values = hidden.astype(jnp.float32)
    mean_square = jnp.mean(values * values, axis=1, keepdims=True)
    return (
        values * lax.rsqrt(mean_square + norm_epsilon) * norm_gain.astype(jnp.float32)[None, :]
    ).astype(jnp.bfloat16)


def quantize(base_rows, low_rank):
    merged = base_rows.astype(jnp.float32) + adapter_scale * low_rank
    row_count, col_count = merged.shape
    tiles = merged.reshape(row_count // BLOCK, BLOCK, col_count // BLOCK, BLOCK)
    largest = jnp.max(jnp.abs(tiles), axis=(1, 3))
    exponent = jnp.ceil(jnp.log2((largest + scale_epsilon) / code_limit))
    scales = jnp.exp2(exponent).astype(jnp.bfloat16)
    quantized = jnp.floor(tiles / scales.astype(jnp.float32)[:, None, :, None] + 0.5).astype(
        jnp.bfloat16
    )
    return (quantized.reshape(row_count, col_count), scales)


def dequantize(quantized, scales):
    row_count, col_count = quantized.shape
    tiles = quantized.reshape(row_count // BLOCK, BLOCK, col_count // BLOCK, BLOCK).astype(
        jnp.float32
    )
    return (
        (tiles * scales.astype(jnp.float32)[:, None, :, None])
        .astype(jnp.bfloat16)
        .reshape(row_count, col_count)
    )


def frequencies(positions):
    pair_index = jnp.arange(HEAD // 2, dtype=jnp.float32)
    inverse = jnp.exp(pair_index * (-2.0 * math.log(rope_theta) / HEAD))
    wavelength = 2.0 * math.pi / inverse
    blend = (initial_context / wavelength - low_factor) / (high_factor - low_factor)
    middle = (1.0 - blend) * inverse / rope_factor + blend * inverse
    adjusted = jnp.where(
        wavelength < initial_context / high_factor,
        inverse,
        jnp.where(wavelength > initial_context / low_factor, inverse / rope_factor, middle),
    )
    angles = positions.astype(jnp.float32)[:, None] * adjusted[None, :]
    return (jnp.cos(angles), jnp.sin(angles))


def rotate(projected, positions):
    cosine, sine_part = frequencies(positions)
    row_count, full_width = projected.shape
    half_head = HEAD // 2
    per_head = projected.reshape(row_count, full_width // HEAD, HEAD)
    first_half = per_head[:, :, :half_head]
    second_half = per_head[:, :, half_head:]
    cosine = cosine[:, None, :]
    sine_part = sine_part[:, None, :]
    turned = jnp.concatenate(
        [
            first_half * cosine - second_half * sine_part,
            second_half * cosine + first_half * sine_part,
        ],
        axis=2,
    )
    return turned.reshape(row_count, full_width)


def shards(hidden, base_weight, adapter_down, adapter_up, norm_gain, positions):
    token_count = hidden.shape[0]
    normed = normalize(hidden, norm_gain)
    low_rank = jnp.dot(adapter_down, adapter_up, preferred_element_type=jnp.float32)
    quantized, scales = quantize(base_weight, low_rank)
    quantized, scales = (
        lax.all_to_all(quantized, "tp", split_axis=1, concat_axis=0, tiled=True),
        lax.all_to_all(scales, "tp", split_axis=1, concat_axis=0, tiled=True),
    )
    weight = dequantize(quantized, scales)
    gathered = lax.all_to_all(normed, "fsdp", split_axis=1, concat_axis=0, tiled=True)
    every_sum = lax.psum(
        jnp.dot(gathered, weight, preferred_element_type=jnp.float32).astype(jnp.bfloat16), "fsdp"
    ).astype(jnp.float32)
    projected = lax.dynamic_slice_in_dim(
        every_sum, lax.axis_index("fsdp") * token_count, token_count, 0
    )
    return rotate(projected, positions).astype(jnp.bfloat16)


def solution(mesh):
    placed = (
        P(("rep", "fsdp"), None),
        P(("rep", "fsdp", "tp"), None),
        P(("rep", "fsdp", "tp"), None),
        P("rep", None),
        P("rep"),
        P(("rep", "fsdp")),
    )
    return jax.shard_map(
        shards, mesh=mesh, in_specs=placed, out_specs=P(("rep", "fsdp"), "tp"), check_vma=False
    )
```

profile of v0, /device:TPU:6, one launch (start us, length us, event | category | flops | bytes accessed | tf_op | source)
XLA Modules:
  0.0 591.6 jit_solution(16495217122207048647)
XLA Ops:
  6.5 0.0 copy-start
  6.5 1.2 copy-done
  7.8 6.9 %abs_reduce_fusion = (f32[16384]{0:T(1024)S(1)}, f32[128,16384]{1,0:T(8,128)}) fusion(bf16[128,32]{0,1:T(8,128)(2,1)} %param.8, bf16[32,16384]{1,0:T(8,128)(2,1)S(1)} %copy-done, bf16[128,16384]{1,0:T(8,128)(2,1)} %param.7), kind=kOutput, calls=%fused_computation.10 | convolution fusion | flops 144687104 | bytes 13705216 | tf_op jit(solution)/shard_map/dot_general | solution.py:93
  14.6 0.1 bitcast_reduce_fusion
  14.8 0.7 reshape.204
  15.5 4.5 all-to-all-start.2
  19.9 0.1 broadcast_bitcast_fusion
  20.0 6.4 %copy.17 = bf16[128,16384]{0,1:T(8,128)(2,1)} copy(bf16[128,16384]{1,0:T(8,128)(2,1)} %param.6) | data formatting | bytes 8388608 | tf_op args[0]
  26.4 3.8 fusion.1
  30.2 0.0 copy-start.2
  30.2 4.1 floor_convert_fusion
  34.2 2.2 copy.34
  36.5 0.0 copy-done.2
  36.5 0.0 all-to-all-done.2
  36.5 4.8 all-to-all-start.1
  41.3 5.8 fusion.3
  47.2 43.9 %all-to-all-done.1 = bf16[128,8,2048]{2,0,1:T(8,128)(2,1)} async-done(((bf16[128,8,2048]{2,0,1:T(8,128)(2,1)}), bf16[128,8,2048]{2,0,1:T(8,128)(2,1)}, u32[]{:S(2)}, u32[]{:S(2)}) %all-to-all-start.1) | async-done | bytes 4194336 | tf_op jit(solution)/shard_map/all_to_all | solution.py:96
  91.1 9.9 %all-to-all-start = ((bf16[128,16,1024]{0,2,1:T(8,128)(2,1)}), bf16[128,16,1024]{0,2,1:T(8,128)(2,1)}, u32[]{:S(2)}, u32[]{:S(2)}) async-start(bf16[128,16,1024]{0,2,1:T(8,128)(2,1)} %bitcast.41), calls=%async_computation | async-start | bytes 8388608 | tf_op jit(solution)/shard_map/all_to_all | solution.py:100
  101.0 0.2 all-reduce.2.cloned.1.call-start
  101.2 3.2 convert_element_type.120
  104.5 2.0 copy.23
  106.5 2.7 fusion.4
  109.2 87.2 %all-to-all-done = bf16[128,16,1024]{0,2,1:T(8,128)(2,1)} async-done(((bf16[128,16,1024]{0,2,1:T(8,128)(2,1)}), bf16[128,16,1024]{0,2,1:T(8,128)(2,1)}, u32[]{:S(2)}, u32[]{:S(2)}) %all-to-all-start) | async-done | bytes 4194336 | tf_op jit(solution)/shard_map/all_to_all | solution.py:100
  196.4 6.4 %copy.18 = bf16[16,128,1024]{2,1,0:T(8,128)(2,1)} copy(bf16[16,128,1024]{1,2,0:T(8,128)(2,1)} %bitcast.1) | data formatting | bytes 8388608 | tf_op jit(solution)/shard_map/all_to_all | solution.py:100
  202.8 14.1 %convolution_convert_fusion = bf16[2048,2048]{1,0:T(8,128)(2,1)} fusion(bf16[2048,1024]{1,0:T(8,128)(2,1)} %bitcast.45, bf16[128,8,16,128]{3,2,1,0:T(8,128)(2,1)} %bitcast.44), kind=kOutput, calls=%fused_computation.11 | convolution fusion | flops 8594128896 | bytes 16777216 | tf_op jit(solution)/shard_map/dot_general | solution.py:102
  216.9 0.0 copy-start.3
  216.9 0.0 copy-start.1
  216.9 0.0 all-reduce.2.cloned.1.call-update
  217.0 0.6 copy-done.3
  217.6 0.3 multiply_cosine_fusion
  217.9 363.7 %all-reduce.2.cloned.1.call-done = bf16[2048,2048]{1,0:T(8,128)(2,1)} async-done(((bf16[2048,2048]{1,0:T(8,128)(2,1)}), bf16[2048,2048]{1,0:T(8,128)(2,1)}) %all-reduce.2.cloned.1.call-update) | async-done | bytes 8388624 | tf_op jit(solution)/shard_map/psum | solution.py:101
  581.6 1.1 convert_bitcast_fusion
  582.8 0.2 copy.25
  583.0 0.5 subtract_convert_fusion
  583.5 0.3 pad_maximum_fusion
  583.8 0.9 copy.35
  584.8 0.0 copy-done.1
  (6 shorter events, 0.1 us)
Async XLA Ops:
  6.5 1.2 copy-start
  15.5 21.0 %all-to-all-start.2 = ((bf16[1,8,16]{2,0,1:T(2,128)(2,1)}), bf16[1,8,16]{2,0,1:T(2,128)(2,1)S(1)}, u32[]{:S(2)}, u32[]{:S(2)}) async-start(bf16[1,8,16]{2,0,1:T(2,128)(2,1)} %reshape.204), calls=%async_computation.2 | async-start | bytes 8192 | tf_op jit(solution)/shard_map/all_to_all | solution.py:97
  30.2 6.3 %copy-start.2 = (bf16[16384]{0:T(1024)(128)(2,1)S(1)}, bf16[16384]{0:T(1024)(128)(2,1)}, u32[]{:S(2)}) copy-start(bf16[16384]{0:T(1024)(128)(2,1)} %param.10) | copy-start | bytes 98308
  36.5 54.6 %all-to-all-start.1 = ((bf16[128,8,2048]{2,0,1:T(8,128)(2,1)}), bf16[128,8,2048]{2,0,1:T(8,128)(2,1)}, u32[]{:S(2)}, u32[]{:S(2)}) async-start(bf16[128,8,2048]{2,0,1:T(8,128)(2,1)} %bitcast.42), calls=%async_computation.1 | async-start | bytes 8388608 | tf_op jit(solution)/shard_map/all_to_all | solution.py:96
  91.1 105.4 %all-to-all-start = ((bf16[128,16,1024]{0,2,1:T(8,128)(2,1)}), bf16[128,16,1024]{0,2,1:T(8,128)(2,1)}, u32[]{:S(2)}, u32[]{:S(2)}) async-start(bf16[128,16,1024]{0,2,1:T(8,128)(2,1)} %bitcast.41), calls=%async_computation | async-start | bytes 8388608 | tf_op jit(solution)/shard_map/all_to_all | solution.py:100
  101.0 480.6 %all-reduce.2.cloned.1.call-start = ((), (), s32[]{:S(2)}) async-start(), calls=%async_computation.3 | async-start | bytes 16777216 | tf_op jit(solution)/shard_map/psum | solution.py:101
  216.9 0.7 copy-start.3
  216.9 367.8 %copy-start.1 = (bf16[32,16384]{1,0:T(8,128)(2,1)S(1)}, bf16[32,16384]{1,0:T(8,128)(2,1)}, u32[]{:S(2)}) copy-start(bf16[32,16384]{1,0:T(8,128)(2,1)} %param.9) | copy-start | bytes 3145732
Sparse Core Ops, SparseCore 0:
  217.1 364.5 all-reduce.1
where the time goes:
time: 594 us; the launch traced here: 592 us
  waiting for transfers between devices  495 us (83%)
  other arithmetic  22.1 us (4%)
  matrix products  21 us (4%)
  local copies, waits for them, and re-layouts  20.8 us (4%)
  starting transfers between devices  19.4 us (3%)
  between operations  13.5 us (2%)
    psum x1, waiting for transfers between devices, shards(): lax.psum(jnp.dot(gathered, weight, preferred_element_type=jnp.float32).as...  364 us
    all_to_all x1, waiting for transfers between devices, shards(): lax.all_to_all(normed, 'fsdp', split_axis=1, concat_axis=0, tiled=True)  87.2 us
    all_to_all x1, waiting for transfers between devices, shards(): lax.all_to_all(quantized, 'tp', split_axis=1, concat_axis=0, tiled=True)  43.9 us
    dot_general x1, matrix products, shards(): jnp.dot(gathered, weight, preferred_element_type=jnp.float32)  14.1 us
  transfers between devices with their start and end apart: 4, of which 3 were waited for; matrix products, arithmetic and copies ran while one was open for 5% of the time, Pallas kernels for 0%

commit v1 on v0

v1 whole, which is shorter than its diff:
```python
import functools
import math

import jax
import jax.numpy as jnp
from jax import lax
from jax.experimental import pallas as pl
from jax.experimental.pallas import tpu as pltpu
from jax.sharding import PartitionSpec as P

HEAD = 128
BLOCK = 128
F32 = jnp.float32
BF16 = jnp.bfloat16

norm_epsilon = 1e-05
scale_epsilon = 1e-06
code_limit = 15.0
adapter_scale = 2.0
rope_theta = 500000.0
rope_factor = 8.0
low_factor = 1.0
high_factor = 4.0
initial_context = 8192.0

NZ = 8
NY = 4
CHUNKS = 4
HALF = NZ // 2
STEPS = NZ - 1


def frequencies(positions):
    pair_index = jnp.arange(HEAD // 2, dtype=F32)
    inverse = jnp.exp(pair_index * (-2.0 * math.log(rope_theta) / HEAD))
    wavelength = 2.0 * math.pi / inverse
    blend = (initial_context / wavelength - low_factor) / (high_factor - low_factor)
    middle = (1.0 - blend) * inverse / rope_factor + blend * inverse
    adjusted = jnp.where(
        wavelength < initial_context / high_factor,
        inverse,
        jnp.where(wavelength > initial_context / low_factor, inverse / rope_factor, middle),
    )
    angles = positions.astype(F32)[:, None] * adjusted[None, :]
    return (jnp.cos(angles), jnp.sin(angles))


def prepare_kernel(steps, hidden_ref, gain_ref, base_ref, down_ref, up_ref, normed_ref, weight_ref, picked, squares):
    step = pl.program_id(0)
    tp = lax.axis_index("tp")
    width = hidden_ref.shape[1]
    values = hidden_ref[...].astype(F32)
    total = None
    for start in range(0, width, 128):
        part = values[:, start : start + 128]
        total = part * part if total is None else total + part * part

    @pl.when(step == 0)
    def _():
        squares[...] = total

    @pl.when(step > 0)
    def _():
        squares[...] += total

    mine = pl.ds(pl.multiple_of(tp * 128, 128), 128)
    picked[step] = hidden_ref[:, mine].astype(F32) * gain_ref[:, mine].astype(F32)

    low_rank = jnp.dot(
        down_ref[...] * adapter_scale, up_ref[...], preferred_element_type=F32
    )
    merged = base_ref[...].astype(F32) + low_rank
    by_column = jnp.max(jnp.abs(merged), axis=0, keepdims=True)
    stacked = jnp.concatenate(
        [by_column[:, start : start + BLOCK] for start in range(0, width, BLOCK)], axis=0
    )
    largest = jnp.max(stacked, axis=1, keepdims=True) + scale_epsilon
    largest = jnp.broadcast_to(largest, stacked.shape)
    scale = jnp.full(stacked.shape, 2.0**-23, F32)
    inverse = jnp.full(stacked.shape, 2.0**23, F32)
    for power in range(-23, 1):
        above = largest > code_limit * 2.0**power
        scale = jnp.where(above, 2.0 ** (power + 1), scale)
        inverse = jnp.where(above, 2.0 ** -(power + 1), inverse)
    for index, start in enumerate(range(0, width, BLOCK)):
        codes = jnp.floor(merged[:, start : start + BLOCK] * inverse[index : index + 1] + 0.5)
        weight_ref[:, start : start + BLOCK] = (codes * scale[index : index + 1]).astype(BF16)

    @pl.when(step == steps - 1)
    def _():
        mean_square = jnp.sum(squares[...], axis=1, keepdims=True) / (steps * width)
        factor = lax.rsqrt(mean_square + norm_epsilon)
        for group in range(steps):
            normed_ref[group * 128 : (group + 1) * 128, :] = (picked[group] * factor).astype(BF16)


def prepare(hidden, gain, base_rows, down, up, groups):
    rows, width = hidden.shape
    block = width // groups
    return pl.pallas_call(
        functools.partial(prepare_kernel, groups),
        grid=(groups,),
        in_specs=[
            pl.BlockSpec((rows, block), lambda i: (0, i)),
            pl.BlockSpec((1, block), lambda i: (0, i)),
            pl.BlockSpec((BLOCK, block), lambda i: (0, i)),
            pl.BlockSpec(down.shape, lambda i: (0, 0)),
            pl.BlockSpec((up.shape[0], block), lambda i: (0, i)),
        ],
        out_specs=[
            pl.BlockSpec((groups * rows, 128), lambda i: (0, 0)),
            pl.BlockSpec((BLOCK, block), lambda i: (0, i)),
        ],
        out_shape=[
            jax.ShapeDtypeStruct((groups * rows, 128), BF16),
            jax.ShapeDtypeStruct((BLOCK, width), BF16),
        ],
        scratch_shapes=[
            pltpu.VMEM((groups, rows, 128), F32),
            pltpu.VMEM((rows, 128), F32),
        ],
        compiler_params=pltpu.CompilerParams(dimension_semantics=("arbitrary",)),
    )(hidden, gain, base_rows, down, up)


def project_kernel(
    n_ref, w_ref, cos_ref, sin_ref, out_ref,
    acts, weights, sums, ring_z, ring_x, swap_x, swap_z,
    local_sem, n_send, n_recv, a_send, a_recv, b_send, b_recv, w_send, w_recv,
    rz_send, rz_recv, rx_send, rx_recv, sx_send, sx_recv, sz_send, sz_recv,
):
    f = lax.axis_index("fsdp")
    t = lax.axis_index("tp")
    z, x = f // 2, f % 2
    y, c = t // 2, t % 2
    peer_x = {"fsdp": z * 2 + (1 - x)}
    place = c * NY + y
    cols = weights.shape[1]
    cw = cols // CHUNKS
    qw = cw // 4

    def zmod(value):
        return (value + 2 * NZ) % NZ

    def remote(src, dst, send, recv, device):
        return pltpu.make_async_remote_copy(
            src_ref=src, dst_ref=dst, send_sem=send, recv_sem=recv,
            device_id=device, device_id_type=pl.DeviceIdType.MESH,
        )

    barrier = pltpu.get_barrier_semaphore()

    @pl.loop(1, 2 * NZ)
    def _(step):
        pl.semaphore_signal(
            barrier, inc=1, device_id={"fsdp": (f + step) % (2 * NZ)},
            device_id_type=pl.DeviceIdType.MESH,
        )

    @pl.loop(1, 2 * NY)
    def _(step):
        pl.semaphore_signal(
            barrier, inc=1, device_id={"tp": (t + step) % (2 * NY)},
            device_id_type=pl.DeviceIdType.MESH,
        )

    pl.semaphore_wait(barrier, 2 * NZ - 1 + 2 * NY - 1)

    def lane(index, size):
        return pl.ds(pl.multiple_of(index * size, size), size)

    my_lane = lane(place, 128)

    def n_copy(source, target):
        return remote(
            n_ref.at[lane(target, 128), :], acts.at[lane(source, 128), my_lane],
            n_send.at[target], n_recv.at[source], {"fsdp": target},
        )

    own_n = pltpu.make_async_copy(
        n_ref.at[lane(f, 128), :], acts.at[lane(f, 128), my_lane], local_sem.at[0]
    )
    own_n.start()

    @pl.loop(1, HALF + 1)
    def _(k):
        for flip in (0, 1):
            n_copy(f, zmod(z + k) * 2 + (x + flip) % 2).start()

            @pl.when(k < HALF)
            def _():
                n_copy(f, zmod(z - k) * 2 + (x + flip) % 2).start()

    n_copy(f, z * 2 + 1 - x).start()

    def w_copy(q, target, source):
        row = (source % 2) * NY + source // 2
        return remote(
            w_ref.at[:, pl.ds(pl.multiple_of(target * cols + q * cw, cw), cw)],
            weights.at[lane(row, BLOCK), lane(q, cw)],
            w_send.at[q, target], w_recv.at[q, source], {"tp": target},
        )

    def w_own(q):
        return pltpu.make_async_copy(
            w_ref.at[:, pl.ds(pl.multiple_of(t * cols + q * cw, cw), cw)],
            weights.at[lane(place, BLOCK), lane(q, cw)], local_sem.at[1 + q],
        )

    def w_start(q):
        for dy, dc in ((1, 0), (3, 0), (1, 1), (3, 1), (2, 0), (2, 1), (0, 1)):
            w_copy(q, ((y + dy) % NY) * 2 + (c + dc) % 2, t).start()
        w_own(q).start()

    w_start(0)

    def block_of(j, which):
        return zmod(z - (j + 1)) if which == 0 else zmod(z + (j + 1) % HALF)

    def a_copy(j, which, source_y, target_y):
        rows = lane(block_of(j, which), 256)
        view = acts.at[rows, lane(c * NY + source_y, 128)]
        return remote(
            view, view, a_send.at[2 * j + which, target_y], a_recv.at[2 * j + which, source_y],
            {"tp": target_y * 2 + c},
        )

    def b_copy(j, which, half):
        view = acts.at[lane(block_of(j, which), 256), lane(half, 128 * NY)]
        return remote(
            view, view, b_send.at[2 * j + which], b_recv.at[2 * j + which], {"tp": y * 2 + 1 - c}
        )

    def stage_a(j):
        for which in (0, 1):
            block = block_of(j, which)
            for other in (0, 1):
                source = block * 2 + other

                @pl.when(source != f)
                def _():
                    n_copy(source, f).wait_recv()

                @pl.when(source == f)
                def _():
                    own_n.wait()

            for dy in (1, 3, 2):
                a_copy(j, which, y, (y + dy) % NY).start()

    def stage_b(j):
        for which in (0, 1):
            for dy in (1, 3, 2):
                a_copy(j, which, (y + dy) % NY, y).wait_recv()
            b_copy(j, which, c).start()

    def stage_c(j):
        for which in (0, 1):
            b_copy(j, which, 1 - c).wait_recv()

    stage_a(0)
    stage_a(1)
    stage_b(0)

    def x_copy(q, j, which):
        rows = pl.ds(pl.multiple_of(block_of(j, which) * 256 + (1 - x) * 128, 128), 128)
        return remote(
            sums.at[rows, pl.ds(pl.multiple_of(q * cw + 2 * qw, qw), 2 * qw)],
            swap_x.at[q, 2 * j + which], sx_send.at[q, 2 * j + which],
            sx_recv.at[q, 2 * j + which], peer_x,
        )

    def products(q, j):
        for which in (0, 1):
            rows = lane(block_of(j, which), 256)
            value = jnp.dot(acts[rows, :], weights[:, lane(q, cw)], preferred_element_type=F32)
            sums[rows, lane(q, cw)] = value.astype(BF16)
            x_copy(q, j, which).start()

    def merge(q, j):
        for which in (0, 1):
            x_copy(q, j, which).wait_recv()
            rows = pl.ds(pl.multiple_of(block_of(j, which) * 256 + x * 128, 128), 128)
            here = pl.ds(pl.multiple_of(q * cw + 2 * qw, qw), 2 * qw)
            sums[rows, here] = (
                sums[rows, here].astype(F32) + swap_x[q, 2 * j + which].astype(F32)
            ).astype(BF16)

    def ring(kind, q, s, way):
        block = zmod(z - 1 - s) if way == 0 else zmod(z + 1 + s)
        target = zmod(z + 1) if way == 0 else zmod(z - 1)
        if kind == 0:
            rows = lane(block, 256)
        else:
            rows = pl.ds(pl.multiple_of(block * 256 + x * 128, 128), 128)
        here = pl.ds(pl.multiple_of(q * cw + (2 * kind + way) * qw, qw), qw)
        slots = ring_z if kind == 0 else ring_x
        sends = rz_send if kind == 0 else rx_send
        recvs = rz_recv if kind == 0 else rx_recv
        view = sums.at[rows, here]

        def hop(step):
            return remote(
                view, slots.at[q, way, step], sends.at[q, way, step], recvs.at[q, way, step],
                {"fsdp": target * 2 + x},
            )

        def arrived():
            hop(s - 1).wait_recv()
            return sums[rows, here].astype(F32) + slots[q, way, s - 1].astype(F32)

        return rows, here, hop, arrived

    def ring_early(kind, q, s):
        for way in (0, 1):
            rows, here, hop, arrived = ring(kind, q, s, way)

            @pl.when(s > 0)
            def _():
                sums[rows, here] = arrived().astype(BF16)

            hop(s).start()

    def finish(q, which, value):
        turned = value * cos_ref[...] + pltpu.roll(value, HEAD // 2, 1) * sin_ref[...]
        out_ref[:, pl.ds(pl.multiple_of(q * cw + which * qw, qw), qw)] = turned.astype(BF16)

    def z_copy(q):
        rows = pl.ds(pl.multiple_of(z * 256 + (1 - x) * 128, 128), 128)
        return remote(
            sums.at[rows, pl.ds(pl.multiple_of(q * cw, cw), 2 * qw)],
            swap_z.at[q], sz_send.at[q], sz_recv.at[q], peer_x,
        )

    def ring_late(kind, q, s):
        for way in (0, 1):
            rows, here, hop, arrived = ring(kind, q, s, way)
            value = arrived()

            @pl.when(s < STEPS)
            def _():
                sums[rows, here] = value.astype(BF16)
                hop(s).start()

            @pl.when(s == STEPS)
            def _():
                if kind == 0:
                    sums[rows, here] = value.astype(BF16)
                else:
                    finish(q, 2 + way, value)

        if kind == 0:

            @pl.when(s == STEPS)
            def _():
                z_copy(q).start()

    def last_z(q):
        z_copy(q).wait_recv()
        rows = pl.ds(pl.multiple_of(z * 256 + x * 128, 128), 128)
        for way in (0, 1):
            here = pl.ds(pl.multiple_of(q * cw + way * qw, qw), qw)
            value = sums[rows, here].astype(F32) + swap_z[q, :, way * qw : (way + 1) * qw].astype(
                F32
            )
            finish(q, way, value)

    @pl.loop(0, HALF * (CHUNKS + 1) + 1)
    def _(r):
        q, j = r // HALF, r % HALF

        @pl.when(r == 0)
        def _():
            stage_a(2)
            stage_b(1)

        @pl.when(r == 1)
        def _():
            stage_a(3)
            stage_b(2)

        @pl.when(r == 2)
        def _():
            stage_b(3)

        @pl.when((r > 0) & (r < CHUNKS))
        def _():
            w_start(r)

        @pl.when(r < HALF)
        def _():
            stage_c(j)

        @pl.when((q >= 2) & (j == 0))
        def _():
            last_z(q - 2)

        q1, j1 = (r + HALF - 1) // HALF - 1, (r + HALF - 1) % HALF

        @pl.when((r >= 1) & (q1 < CHUNKS))
        def _():
            merge(q1, j1)
            ring_early(1, q1, j1)

        @pl.when(q1 >= 1)
        def _():
            ring_late(1, q1 - 1, j1 + HALF)

        @pl.when((q < CHUNKS) & (j == 0))
        def _():
            w_own(q).wait()

            @pl.loop(1, 2 * NY)
            def _(step):
                w_copy(q, t, (t + step) % (2 * NY)).wait_recv()

        @pl.when(q < CHUNKS)
        def _():
            products(q, j)
            ring_early(0, q, j)

        @pl.when((q >= 1) & (q <= CHUNKS))
        def _():
            ring_late(0, q - 1, j + HALF)

    @pl.loop(1, 2 * NZ)
    def _(step):
        n_copy(f, (f + step) % (2 * NZ)).wait_send()

    @pl.loop(0, HALF)
    def _(j):
        for which in (0, 1):
            for dy in (1, 2, 3):
                a_copy(j, which, y, (y + dy) % NY).wait_send()
            b_copy(j, which, c).wait_send()

    @pl.loop(0, CHUNKS)
    def _(q):
        @pl.loop(1, 2 * NY)
        def _(step):
            w_copy(q, (t + step) % (2 * NY), t).wait_send()

        @pl.loop(0, HALF)
        def _(j):
            for which in (0, 1):
                x_copy(q, j, which).wait_send()

        @pl.loop(0, STEPS)
        def _(s):
            for kind in (0, 1):
                for way in (0, 1):
                    ring(kind, q, s, way)[2](s).wait_send()

        z_copy(q).wait_send()


def project(normed, weight, cosine, sine, groups, members):
    width = weight.shape[1]
    cols = width // members
    tokens = groups * 128
    cw = cols // CHUNKS
    qw = cw // 4
    dma = pltpu.SemaphoreType.DMA
    any_spec = pl.BlockSpec(memory_space=pl.ANY)
    vmem_spec = pl.BlockSpec(memory_space=pltpu.VMEM)
    return pl.pallas_call(
        project_kernel,
        in_specs=[any_spec, any_spec, vmem_spec, vmem_spec],
        out_specs=vmem_spec,
        out_shape=jax.ShapeDtypeStruct((128, cols), BF16),
        scratch_shapes=[
            pltpu.VMEM((tokens, members * BLOCK), BF16),
            pltpu.VMEM((members * BLOCK, cols), BF16),
            pltpu.VMEM((tokens, cols), BF16),
            pltpu.VMEM((CHUNKS, 2, STEPS, 256, qw), BF16),
            pltpu.VMEM((CHUNKS, 2, STEPS, 128, qw), BF16),
            pltpu.VMEM((CHUNKS, NZ, 128, 2 * qw), BF16),
            pltpu.VMEM((CHUNKS, 128, 2 * qw), BF16),
            dma((1 + CHUNKS,)),
            dma((groups,)), dma((groups,)),
            dma((NZ, NY)), dma((NZ, NY)),
            dma((NZ,)), dma((NZ,)),
            dma((CHUNKS, members)), dma((CHUNKS, members)),
            dma((CHUNKS, 2, STEPS)), dma((CHUNKS, 2, STEPS)),
            dma((CHUNKS, 2, STEPS)), dma((CHUNKS, 2, STEPS)),
            dma((CHUNKS, NZ)), dma((CHUNKS, NZ)),
            dma((CHUNKS,)), dma((CHUNKS,)),
        ],
        compiler_params=pltpu.CompilerParams(
            collective_id=0, has_side_effects=True, vmem_limit_bytes=48 * 1024 * 1024
        ),
    )(normed, weight, cosine, sine)


def solution(mesh):
    groups, members = mesh.shape["fsdp"], mesh.shape["tp"]

    def shards(hidden, base_weight, adapter_down, adapter_up, norm_gain, positions):
        normed, weight = prepare(
            hidden, norm_gain[None, :], base_weight, adapter_down, adapter_up, groups
        )
        cosine, sine = frequencies(positions)
        return project(
            normed, weight,
            jnp.concatenate([cosine, cosine], axis=1),
            jnp.concatenate([-sine, sine], axis=1),
            groups, members,
        )

    placed = (
        P(("rep", "fsdp"), None),
        P(("rep", "fsdp", "tp"), None),
        P(("rep", "fsdp", "tp"), None),
        P("rep", None),
        P("rep"),
        P(("rep", "fsdp")),
    )
    return jax.shard_map(
        shards, mesh=mesh, in_specs=placed, out_specs=P(("rep", "fsdp"), "tp"), check_vma=False
    )
```

time: 594 us -> 166 us (0.28)
  waiting for transfers between devices: 495 us -> 0 us
  Pallas kernels: 0 us -> 156 us
  other arithmetic: 22.1 us -> 1.08 us
  matrix products: 21 us -> 0 us
  starting transfers between devices: 19.4 us -> 0 us
  local copies, waits for them, and re-layouts: 20.8 us -> 6.85 us
  between operations: 13.5 us -> 0.03 us
    psum x1 -> x0, waiting for transfers between devices: 364 us -> none  [shards(): lax.psum(jnp.dot(gathered, weight, preferred_element_type=jnp.float32).as...]
    pallas_call x0 -> x2, Pallas kernels: none -> 156 us  [the longest x1 142 us: project(): pl.pallas_call(project_kernel, in_specs=[any_spec, any_spec, vmem_spec, v...]
    all_to_all x3 -> x0, waiting for transfers between devices: 131 us -> none  [the longest x1 87.2 us: shards(): lax.all_to_all(normed, 'fsdp', split_axis=1, concat_axis=0, tiled=True)]
    dot_general x2 -> x0, matrix products: 21 us -> none  [the longest x1 14.1 us: shards(): jnp.dot(gathered, weight, preferred_element_type=jnp.float32)]
    all_to_all x3 -> x0, starting transfers between devices: 19.2 us -> none  [the longest x1 9.94 us: shards(): lax.all_to_all(normed, 'fsdp', split_axis=1, concat_axis=0, tiled=True)]
    convert_element_type x8 -> x1, other arithmetic: 15.9 us -> 0.66 us  [frequencies(): angles = positions.astype(F32)[:, None] * adjusted[None, :]]
    all_to_all x2 -> x0, local copies, waits for them, and re-layouts: 8.63 us -> none  [the longest x1 6.39 us: shards(): lax.all_to_all(normed, 'fsdp', split_axis=1, concat_axis=0, tiled=True)]
  transfers between devices with their start and end apart: 4 -> 0, of which waited for: 3 -> 0; matrix products, arithmetic and copies ran while one was open for 5% -> 0% of each run, Pallas kernels for 0% -> 0%
where the time goes in v1:
time: 166 us; the launch traced here: 164 us
  Pallas kernels  156 us (94%)
  local copies, waits for them, and re-layouts  6.85 us (4%)
    pallas_call x1, Pallas kernels, project(): pl.pallas_call(project_kernel, in_specs=[any_spec, any_spec, vmem_spec, v...  142 us
    pallas_call x1, Pallas kernels, prepare(): pl.pallas_call(functools.partial(prepare_kernel, groups), grid=(groups,),...  14.8 us
    unnamed x6, local copies, waits for them, and re-layouts  5.43 us

profile of v1, /device:TPU:6, one launch (start us, length us, event | category | flops | bytes accessed | tf_op | source)
XLA Modules:
  0.0 164.3 jit_solution(13415856693325893217)
XLA Ops:
  0.0 0.7 convert_element_type.3
  0.7 1.4 copy.7.down_ref
  2.1 1.4 broadcast_in_dim.2.gain_ref
  3.5 0.3 fusion
  3.8 0.1 pad_maximum_fusion
  3.9 14.8 %shard_map.64 = (bf16[2048,128]{1,0:T(8,128)(2,1)}, bf16[128,16384]{1,0:T(8,128)(2,1)}) custom-call(bf16[128,16384]{1,0:T(8,128)(2,1)} %hidden_ref.1, bf16[1,16384]{1,0:T(2,128)(2,1)} %broadcast_in_dim.2.gain_ref, bf16[128,16384]{1,0:T(8,128)(2,1)} %base_ref.1, bf16[128,32]{1,0:T(8,128)(2,1)} %copy.7.down_ref, bf16[32,16384]{1,0:T(8,128)(2,1)} %up_ref.1), custom_call_target="tpu_custom_call" | custom-call | tf_op jit(solution)/shard_map/pallas_call | solution.py:100
  18.7 0.0 copy-start
  18.7 2.2 %copy-done = bf16[128,16384]{1,0:T(8,128)(2,1)S(1)} copy-done((bf16[128,16384]{1,0:T(8,128)(2,1)S(1)}, bf16[128,16384]{1,0:T(8,128)(2,1)}, u32[]{:S(2)}) %copy-start) | copy-done | bytes 4194328
  20.9 0.0 copy-start.1
  20.9 1.0 copy-done.1
  22.0 141.6 %shard_map.65 = bf16[128,2048]{1,0:T(8,128)(2,1)S(1)} custom-call(bf16[2048,128]{1,0:T(8,128)(2,1)S(1)} %copy-done.1, bf16[128,16384]{1,0:T(8,128)(2,1)S(1)} %copy-done, f32[128,128]{1,0:T(8,128)S(1)} %get-tuple-element.12.cos_ref, f32[128,128]{1,0:T(8,128)S(1)} %get-tuple-element.13.sin_ref), custom_call_target="tpu_custom_call" | custom-call | tf_op jit(solution)/shard_map/pallas_call | solution.py:466
  163.5 0.8 copy.9
  (1 shorter events, 0.0 us)
Async XLA Ops:
  18.7 2.2 %copy-start = (bf16[128,16384]{1,0:T(8,128)(2,1)S(1)}, bf16[128,16384]{1,0:T(8,128)(2,1)}, u32[]{:S(2)}) copy-start(bf16[128,16384]{1,0:T(8,128)(2,1)} %get-tuple-element.8.w_ref) | copy-start | bytes 12582916
  20.9 1.0 copy-start.1

commit v2 on v0

v2 whole, which is shorter than its diff:
```python
import functools
import math

import jax
import jax.numpy as jnp
from jax import lax
from jax.experimental import pallas as pl
from jax.experimental.pallas import tpu as pltpu
from jax.sharding import PartitionSpec as P

HEAD = 128
BLOCK = 128
F32 = jnp.float32
BF16 = jnp.bfloat16

norm_epsilon = 1e-05
scale_epsilon = 1e-06
code_limit = 15.0
adapter_scale = 2.0
rope_theta = 500000.0
rope_factor = 8.0
low_factor = 1.0
high_factor = 4.0
initial_context = 8192.0

NZ = 8
NY = 4
CHUNKS = 8
STRIDE = 2
LAST = NZ // 2
OFFSETS = (4, 3, -3, 2, -2, 1, -1, 0)
STEP_BLOCKS = ((0,), (1, 2), (3, 4), (5, 6), (7,))


def frequencies(positions):
    pair_index = jnp.arange(HEAD // 2, dtype=F32)
    inverse = jnp.exp(pair_index * (-2.0 * math.log(rope_theta) / HEAD))
    wavelength = 2.0 * math.pi / inverse
    blend = (initial_context / wavelength - low_factor) / (high_factor - low_factor)
    middle = (1.0 - blend) * inverse / rope_factor + blend * inverse
    adjusted = jnp.where(
        wavelength < initial_context / high_factor,
        inverse,
        jnp.where(wavelength > initial_context / low_factor, inverse / rope_factor, middle),
    )
    angles = positions.astype(F32)[:, None] * adjusted[None, :]
    return (jnp.cos(angles), jnp.sin(angles))


def project_kernel(
    hidden_hbm, base_hbm, gain_ref, down_ref, up_ref, cos_ref, sin_ref, out_ref,
    hidden, base, normed, coded, acts, weights, sums, ring_z, ring_x, swap_x, swap_z,
    load_sem, local_sem, n_send, n_recv, a_send, a_recv, h_send, h_recv, b_send, b_recv,
    w_send, w_recv, rz_send, rz_recv, rx_send, rx_recv, sx_send, sx_recv, sz_send, sz_recv,
):
    f = lax.axis_index("fsdp")
    t = lax.axis_index("tp")
    z, x = f // 2, f % 2
    y, c = t // 2, t % 2
    peer_x = {"fsdp": z * 2 + (1 - x)}
    place = c * NY + y
    cols = weights.shape[1]
    cw = cols // CHUNKS
    tile = cw // 2
    groups = 2 * NZ
    width = hidden.shape[1]

    load_hidden = pltpu.make_async_copy(hidden_hbm, hidden, load_sem.at[0])
    load_base = pltpu.make_async_copy(base_hbm, base, load_sem.at[1])
    load_hidden.start()
    load_base.start()

    def zmod(value):
        return (value + NZ) % NZ

    def remote(src, dst, send, recv, device):
        return pltpu.make_async_remote_copy(
            src_ref=src, dst_ref=dst, send_sem=send, recv_sem=recv,
            device_id=device, device_id_type=pl.DeviceIdType.MESH,
        )

    def lane(index, size):
        return pl.ds(pl.multiple_of(index * size, size), size)

    barrier = pltpu.get_barrier_semaphore()

    @pl.loop(1, groups)
    def _(step):
        pl.semaphore_signal(
            barrier, inc=1, device_id={"fsdp": (f + step) % groups},
            device_id_type=pl.DeviceIdType.MESH,
        )

    @pl.loop(1, 2 * NY)
    def _(step):
        pl.semaphore_signal(
            barrier, inc=1, device_id={"tp": (t + step) % (2 * NY)},
            device_id_type=pl.DeviceIdType.MESH,
        )

    load_hidden.wait()
    span = width // groups

    def squares(group, total):
        values = hidden[:, lane(group, span)].astype(F32)
        for start in range(0, span, 128):
            part = values[:, start : start + 128]
            total = total + part * part
        return total

    total = lax.fori_loop(0, groups, squares, jnp.zeros((128, 128), F32))
    mean_square = jnp.sum(total, axis=1, keepdims=True) / width
    factor = jnp.broadcast_to(lax.rsqrt(mean_square + norm_epsilon), (128, 128))

    @pl.loop(0, groups)
    def _(group):
        mine = lane(group * (span // 128) + t, 128)
        normed[lane(group, 128), :] = (
            hidden[:, mine].astype(F32) * factor * gain_ref[:, mine].astype(F32)
        ).astype(BF16)

    pl.semaphore_wait(barrier, groups - 1 + 2 * NY - 1)

    def n_copy(source, target):
        return remote(
            normed.at[lane(target, 128), :], acts.at[lane(source, 128), lane(place, 128)],
            n_send.at[target], n_recv.at[source], {"fsdp": target},
        )

    own_n = pltpu.make_async_copy(
        normed.at[lane(f, 128), :], acts.at[lane(f, 128), lane(place, 128)], local_sem.at[0]
    )
    for offset in OFFSETS[:-1]:
        for flip in (0, 1):
            n_copy(f, zmod(z - offset) * 2 + (x + flip) % 2).start()
    n_copy(f, z * 2 + 1 - x).start()
    own_n.start()

    def w_copy(q, target, source):
        row = (source % 2) * NY + source // 2
        return remote(
            coded.at[:, pl.ds(pl.multiple_of(target * cols + q * cw, cw), cw)],
            weights.at[lane(row, BLOCK), lane(q, cw)],
            w_send.at[q, target], w_recv.at[q, source], {"tp": target},
        )

    def w_own(q):
        return pltpu.make_async_copy(
            coded.at[:, pl.ds(pl.multiple_of(t * cols + q * cw, cw), cw)],
            weights.at[lane(place, BLOCK), lane(q, cw)], local_sem.at[1 + q],
        )

    def w_start(q):
        @pl.loop(0, 2 * NY)
        def _(target):
            here = pl.ds(pl.multiple_of(target * cols + q * cw, cw), cw)
            low_rank = lax.dot_general(
                down_ref[...] * adapter_scale, up_ref[:, here], (((0,), (0,)), ((), ())),
                preferred_element_type=F32,
            )
            merged = base[:, here].astype(F32) + low_rank
            by_column = jnp.max(jnp.abs(merged), axis=0, keepdims=True)
            stacked = jnp.concatenate(
                [by_column[:, start : start + BLOCK] for start in range(0, cw, BLOCK)], axis=0
            )
            largest = jnp.max(stacked, axis=1, keepdims=True) + scale_epsilon
            largest = jnp.broadcast_to(largest, stacked.shape)
            scale = jnp.full(stacked.shape, 2.0**-23, F32)
            inverse = jnp.full(stacked.shape, 2.0**23, F32)
            for power in range(-23, 1):
                above = largest > code_limit * 2.0**power
                scale = jnp.where(above, 2.0 ** (power + 1), scale)
                inverse = jnp.where(above, 2.0 ** -(power + 1), inverse)
            result = []
            for index, start in enumerate(range(0, cw, BLOCK)):
                codes = jnp.floor(
                    merged[:, start : start + BLOCK] * inverse[index : index + 1] + 0.5
                )
                result.append((codes * scale[index : index + 1]).astype(BF16))
            coded[:, here] = jnp.concatenate(result, axis=1)

        for dy, dc in ((1, 0), (3, 0), (1, 1), (3, 1), (2, 0), (2, 1), (0, 1)):
            w_copy(q, ((y + dy) % NY) * 2 + (c + dc) % 2, t).start()
        w_own(q).start()

    def rows_of(i):
        return lane(zmod(z + OFFSETS[i]), 256)

    def a_copy(i, source_y, way):
        view = acts.at[rows_of(i), lane(c * NY + source_y, 128)]
        target = (y + (1 if way == 0 else NY - 1)) % NY
        return remote(view, view, a_send.at[i, way], a_recv.at[i, way], {"tp": target * 2 + c})

    def h_copy(i, source_y, way):
        rows = pl.ds(pl.multiple_of(zmod(z + OFFSETS[i]) * 256 + way * 128, 128), 128)
        view = acts.at[rows, lane(c * NY + source_y, 128)]
        target = (y + (1 if way == 0 else NY - 1)) % NY
        return remote(view, view, h_send.at[i, way], h_recv.at[i, way], {"tp": target * 2 + c})

    def b_copy(i, half):
        view = acts.at[rows_of(i), lane(half, 128 * NY)]
        return remote(view, view, b_send.at[i], b_recv.at[i], {"tp": y * 2 + 1 - c})

    down_y, up_y, far_y = (y + NY - 1) % NY, (y + 1) % NY, (y + 2) % NY

    def stage_a(i):
        block = zmod(z + OFFSETS[i])
        if OFFSETS[i]:
            for other in (0, 1):
                n_copy(block * 2 + other, f).wait_recv()
        else:
            n_copy(z * 2 + 1 - x, f).wait_recv()
            own_n.wait()
        for way in (0, 1):
            a_copy(i, y, way).start()

    def stage_h(i):
        for way, source in ((0, down_y), (1, up_y)):
            a_copy(i, source, way).wait_recv()
            h_copy(i, source, way).start()

    def stage_b(i):
        for way in (0, 1):
            h_copy(i, far_y, way).wait_recv()
        b_copy(i, c).start()

    def stage_c(i):
        b_copy(i, 1 - c).wait_recv()

    def x_copy(q, i):
        rows = pl.ds(pl.multiple_of(zmod(z + OFFSETS[i]) * 256 + (1 - x) * 128, 128), 128)
        here = pl.ds(pl.multiple_of(q * cw + tile, tile), tile)
        return remote(
            sums.at[rows, here], swap_x.at[q, i], sx_send.at[q, i], sx_recv.at[q, i], peer_x
        )

    def products(q, s):
        for i in STEP_BLOCKS[s]:
            value = jnp.dot(
                acts[rows_of(i), :], weights[:, lane(q, cw)], preferred_element_type=F32
            )
            sums[rows_of(i), lane(q, cw)] = value.astype(BF16)
            x_copy(q, i).start()

    def finish(q, which, value):
        turned = value * cos_ref[...] + pltpu.roll(value, HEAD // 2, 1) * sin_ref[...]
        out_ref[:, pl.ds(pl.multiple_of(q * cw + which * tile, tile), tile)] = turned.astype(BF16)

    def z_copy(q):
        rows = pl.ds(pl.multiple_of(z * 256 + (1 - x) * 128, 128), 128)
        return remote(
            sums.at[rows, pl.ds(pl.multiple_of(q * cw, cw), tile)],
            swap_z.at[q], sz_send.at[q], sz_recv.at[q], peer_x,
        )

    def ring(kind, q, s, way):
        size = 256 if kind == 0 else 128
        block = zmod(z + (LAST - s)) if way == 0 else zmod(z - (LAST - s))
        first = block * 256 if kind == 0 else block * 256 + x * 128
        here = pl.ds(pl.multiple_of(q * cw + kind * tile, tile), tile)
        slots, sends, recvs = (
            (ring_z, rz_send, rz_recv) if kind == 0 else (ring_x, rx_send, rx_recv)
        )
        target = zmod(z + 1) if way == 0 else zmod(z - 1)

        def hop(step):
            if step == 0:
                half = size // 2
                src = sums.at[pl.ds(pl.multiple_of(first + way * half, half), half), here]
                dst = slots.at[q, way, 0, pl.ds(0, half)]
            else:
                src = sums.at[pl.ds(pl.multiple_of(first, size), size), here]
                dst = slots.at[q, way, step]
            return remote(
                src, dst, sends.at[q, way, step], recvs.at[q, way, step],
                {"fsdp": target * 2 + x},
            )

        return size, first, here, slots, hop

    def ring_step(kind, q, s):
        size, first, here, slots, hop = ring(kind, q, s, 0)
        half = size // 2

        def read(start, count):
            rows = pl.ds(pl.multiple_of(start, count), count)
            return sums[rows, here].astype(F32)

        def put(start, count, value):
            sums[pl.ds(pl.multiple_of(start, count), count), here] = value.astype(BF16)

        def swapped(i, start=0, count=size):
            return swap_x[q, i, start : start + count].astype(F32)

        if kind == 1:
            for i in STEP_BLOCKS[s]:
                x_copy(q, i).wait_recv()
        if s == 0:
            if kind == 1:
                put(first, size, read(first, size) + swapped(0))
            for way in (0, 1):
                ring(kind, q, s, way)[4](0).start()
        elif s < LAST:
            for way in (0, 1):
                size, first, here, slots, hop = ring(kind, q, s, way)
                i = STEP_BLOCKS[s][way]
                hop(s - 1).wait_recv()
                if s == 1:
                    near = first + way * half
                    value = read(near, half) + slots[q, way, 0, 0:half].astype(F32)
                    if kind == 1:
                        value = value + swapped(i, way * half, half)
                        other = first + (1 - way) * half
                        put(other, half, read(other, half) + swapped(i, (1 - way) * half, half))
                    put(near, half, value)
                else:
                    value = read(first, size) + slots[q, way, s - 1].astype(F32)
                    if kind == 1:
                        value = value + swapped(i)
                    put(first, size, value)
                hop(s).start()
        else:
            value = read(first, size)
            if kind == 1:
                value = value + swapped(7)
            for way in (0, 1):
                ring(kind, q, s, way)[4](s - 1).wait_recv()
                value = value + slots[q, way, s - 1].astype(F32)
            if kind == 0:
                put(first, size, value)
                z_copy(q).start()
            else:
                finish(q, 1, value)

    def last_z(q):
        z_copy(q).wait_recv()
        rows = pl.ds(pl.multiple_of(z * 256 + x * 128, 128), 128)
        here = pl.ds(pl.multiple_of(q * cw, cw), tile)
        finish(q, 0, sums[rows, here].astype(F32) + swap_z[q].astype(F32))

    load_base.wait()
    w_start(0)
    stage_a(0)
    w_start(1)
    stage_a(1), stage_a(2), stage_h(0)
    stage_a(3), stage_a(4), stage_h(1), stage_h(2), stage_b(0)
    stage_a(5), stage_a(6), stage_h(3), stage_h(4), stage_b(1), stage_b(2)
    stage_a(7), stage_h(5), stage_h(6), stage_b(3), stage_b(4)
    stage_h(7), stage_b(5), stage_b(6)

    def at_chunk(start, run):
        @pl.when((start >= 0) & (start % STRIDE == 0) & (start < STRIDE * CHUNKS))
        def _():
            run(start // STRIDE)

    @pl.loop(0, STRIDE * (CHUNKS - 1) + LAST + 3)
    def _(r):
        at_chunk(r - LAST - 2, last_z)
        for s in range(LAST, -1, -1):
            at_chunk(r - s - 1, functools.partial(ring_step, 0, s=s))
            at_chunk(r - s - 2, functools.partial(ring_step, 1, s=s))

        @pl.when(r == 0)
        def _():
            stage_b(7)

        @pl.when(r + 2 < CHUNKS)
        def _():
            w_start(r + 2)

        for s in range(LAST + 1):

            @pl.when(r == s)
            def _():
                for i in STEP_BLOCKS[s]:
                    stage_c(i)

        def arrive(q):
            w_own(q).wait()

            @pl.loop(1, 2 * NY)
            def _(step):
                w_copy(q, t, (t + step) % (2 * NY)).wait_recv()

        at_chunk(r, arrive)
        for s in range(LAST, -1, -1):
            at_chunk(r - s, functools.partial(products, s=s))

    @pl.loop(1, groups)
    def _(step):
        n_copy(f, (f + step) % groups).wait_send()

    for i in range(NZ):
        for way in (0, 1):
            a_copy(i, y, way).wait_send()
            h_copy(i, y, way).wait_send()
        b_copy(i, c).wait_send()

    @pl.loop(0, CHUNKS)
    def _(q):
        @pl.loop(1, 2 * NY)
        def _(step):
            w_copy(q, (t + step) % (2 * NY), t).wait_send()

        for i in range(NZ):
            x_copy(q, i).wait_send()
        for kind in (0, 1):
            for way in (0, 1):
                for s in range(LAST):
                    ring(kind, q, s, way)[4](s).wait_send()
        z_copy(q).wait_send()


def project(hidden, base, gain, down, up, cosine, sine, groups, members):
    width = base.shape[1]
    cols = width // members
    tokens = groups * 128
    tile = cols // CHUNKS // 2
    dma = pltpu.SemaphoreType.DMA
    any_spec = pl.BlockSpec(memory_space=pl.ANY)
    vmem_spec = pl.BlockSpec(memory_space=pltpu.VMEM)
    pair = lambda *shape: [dma(shape), dma(shape)]
    return pl.pallas_call(
        project_kernel,
        in_specs=[any_spec, any_spec] + [vmem_spec] * 5,
        out_specs=vmem_spec,
        out_shape=jax.ShapeDtypeStruct((128, cols), BF16),
        scratch_shapes=[
            pltpu.VMEM((128, width), BF16),
            pltpu.VMEM((128, width), BF16),
            pltpu.VMEM((tokens, 128), BF16),
            pltpu.VMEM((128, width), BF16),
            pltpu.VMEM((tokens, members * BLOCK), BF16),
            pltpu.VMEM((members * BLOCK, cols), BF16),
            pltpu.VMEM((tokens, cols), BF16),
            pltpu.VMEM((CHUNKS, 2, LAST, 256, tile), BF16),
            pltpu.VMEM((CHUNKS, 2, LAST, 128, tile), BF16),
            pltpu.VMEM((CHUNKS, NZ, 128, tile), BF16),
            pltpu.VMEM((CHUNKS, 128, tile), BF16),
            dma((2,)),
            dma((1 + CHUNKS,)),
            *pair(groups),
            *pair(NZ, 2),
            *pair(NZ, 2),
            *pair(NZ),
            *pair(CHUNKS, members),
            *pair(CHUNKS, 2, LAST),
            *pair(CHUNKS, 2, LAST),
            *pair(CHUNKS, NZ),
            *pair(CHUNKS),
        ],
        compiler_params=pltpu.CompilerParams(
            collective_id=0, has_side_effects=True, vmem_limit_bytes=60 * 1024 * 1024
        ),
    )(hidden, base, gain, down, up, cosine, sine)


def solution(mesh):
    groups, members = mesh.shape["fsdp"], mesh.shape["tp"]

    def shards(hidden, base_weight, adapter_down, adapter_up, norm_gain, positions):
        cosine, sine = frequencies(positions)
        return project(
            hidden, base_weight, norm_gain[None, :], adapter_down.T, adapter_up,
            jnp.concatenate([cosine, cosine], axis=1),
            jnp.concatenate([-sine, sine], axis=1),
            groups, members,
        )

    placed = (
        P(("rep", "fsdp"), None),
        P(("rep", "fsdp", "tp"), None),
        P(("rep", "fsdp", "tp"), None),
        P("rep", None),
        P("rep"),
        P(("rep", "fsdp")),
    )
    return jax.shard_map(
        shards, mesh=mesh, in_specs=placed, out_specs=P(("rep", "fsdp"), "tp"), check_vma=False
    )
```

time: 594 us -> 151 us (0.25)
  waiting for transfers between devices: 495 us -> 0 us
  Pallas kernels: 0 us -> 146 us
  matrix products: 21 us -> 0 us
  other arithmetic: 22.1 us -> 1.74 us
  starting transfers between devices: 19.4 us -> 0 us
  local copies, waits for them, and re-layouts: 20.8 us -> 3.31 us
  between operations: 13.5 us -> 0.02 us
    psum x1 -> x0, waiting for transfers between devices: 364 us -> none  [shards(): lax.psum(jnp.dot(gathered, weight, preferred_element_type=jnp.float32).as...]
    pallas_call x0 -> x1, Pallas kernels: none -> 146 us  [project(): pl.pallas_call(project_kernel, in_specs=[any_spec, any_spec] + [vmem_spec...]
    all_to_all x3 -> x0, waiting for transfers between devices: 131 us -> none  [the longest x1 87.2 us: shards(): lax.all_to_all(normed, 'fsdp', split_axis=1, concat_axis=0, tiled=True)]
    dot_general x2 -> x0, matrix products: 21 us -> none  [the longest x1 14.1 us: shards(): jnp.dot(gathered, weight, preferred_element_type=jnp.float32)]
    all_to_all x3 -> x0, starting transfers between devices: 19.2 us -> none  [the longest x1 9.94 us: shards(): lax.all_to_all(normed, 'fsdp', split_axis=1, concat_axis=0, tiled=True)]
    convert_element_type x8 -> x1, other arithmetic: 15.9 us -> 0.66 us  [frequencies(): angles = positions.astype(F32)[:, None] * adjusted[None, :]]
    unnamed x12 -> x1, local copies, waits for them, and re-layouts: 11.3 us -> 1.88 us
    all_to_all x2 -> x0, local copies, waits for them, and re-layouts: 8.63 us -> none  [the longest x1 6.39 us: shards(): lax.all_to_all(normed, 'fsdp', split_axis=1, concat_axis=0, tiled=True)]
  transfers between devices with their start and end apart: 4 -> 0, of which waited for: 3 -> 0; matrix products, arithmetic and copies ran while one was open for 5% -> 0% of each run, Pallas kernels for 0% -> 0%
where the time goes in v2:
time: 151 us
  Pallas kernels  146 us (97%)
  local copies, waits for them, and re-layouts  3.31 us (2%)
  other arithmetic  1.74 us (1%)
    pallas_call x1, Pallas kernels, project(): pl.pallas_call(project_kernel, in_specs=[any_spec, any_spec] + [vmem_spec...  146 us

profile of v2, /device:TPU:6, one launch (start us, length us, event | category | flops | bytes accessed | tf_op | source)
XLA Modules:
  0.0 150.8 jit_solution(5057458375302991450)
XLA Ops:
  0.0 0.7 convert_element_type.3
  0.7 1.4 broadcast_in_dim.2.gain_ref
  2.1 0.3 fusion
  2.4 0.8 pad_maximum_fusion
  3.2 145.7 %shard_map.64 = bf16[128,2048]{1,0:T(8,128)(2,1)} custom-call(bf16[128,16384]{1,0:T(8,128)(2,1)} %hidden_hbm.1, bf16[128,16384]{1,0:T(8,128)(2,1)} %base_hbm.1, bf16[1,16384]{1,0:T(2,128)(2,1)} %broadcast_in_dim.2.gain_ref, bf16[32,128]{1,0:T(8,128)(2,1)} %bitcast.1, bf16[32,16384]{1,0:T(8,128)(2,1)} %up_ref.1, f32[128,128]{1,0:T(8,128)} %get-tuple-element.8.cos_ref, ...), custom_call_target="tpu_custom_call" | custom-call | tf_op jit(solution)/shard_map/pallas_call | solution.py:423
  148.9 1.9 %copy.8 = bf16[128,2048]{1,0:T(8,128)(2,1)} copy(bf16[128,2048]{1,0:T(8,128)(2,1)} %shard_map.64) | data formatting | bytes 1048576
  (1 shorter events, 0.0 us)

commit v3 on v2

--- a/solution.py
+++ b/solution.py
@@ -26,7 +26,7 @@
 NZ = 8
 NY = 4
 CHUNKS = 8
-STRIDE = 2
+STRIDE = 1
 LAST = NZ // 2
 OFFSETS = (4, 3, -3, 2, -2, 1, -1, 0)
 STEP_BLOCKS = ((0,), (1, 2), (3, 4), (5, 6), (7,))
@@ -110,14 +110,16 @@
 
     total = lax.fori_loop(0, groups, squares, jnp.zeros((128, 128), F32))
     mean_square = jnp.sum(total, axis=1, keepdims=True) / width
+    members = 2 * NY
+    chosen = lax.broadcasted_iota(jnp.int32, (members, 128), 0) == t
     factor = jnp.broadcast_to(lax.rsqrt(mean_square + norm_epsilon), (128, 128))
 
     @pl.loop(0, groups)
     def _(group):
-        mine = lane(group * (span // 128) + t, 128)
-        normed[lane(group, 128), :] = (
-            hidden[:, mine].astype(F32) * factor * gain_ref[:, mine].astype(F32)
-        ).astype(BF16)
+        mine = lane(group * members + t, 128)
+        gains = gain_ref[lane(group, members), :].astype(F32)
+        gain = jnp.sum(jnp.where(chosen, gains, 0.0), axis=0, keepdims=True)
+        normed[lane(group, 128), :] = (hidden[:, mine].astype(F32) * factor * gain).astype(BF16)
 
     pl.semaphore_wait(barrier, groups - 1 + 2 * NY - 1)
 
@@ -151,33 +153,35 @@
         )
 
     def w_start(q):
-        @pl.loop(0, 2 * NY)
-        def _(target):
+        doubled = down_ref[...] * adapter_scale
+        views, merged, maxima = [], [], []
+        for target in range(2 * NY):
             here = pl.ds(pl.multiple_of(target * cols + q * cw, cw), cw)
             low_rank = lax.dot_general(
-                down_ref[...] * adapter_scale, up_ref[:, here], (((0,), (0,)), ((), ())),
-                preferred_element_type=F32,
+                doubled, up_ref[:, here], (((0,), (0,)), ((), ())), preferred_element_type=F32
             )
-            merged = base[:, here].astype(F32) + low_rank
-            by_column = jnp.max(jnp.abs(merged), axis=0, keepdims=True)
-            stacked = jnp.concatenate(
-                [by_column[:, start : start + BLOCK] for start in range(0, cw, BLOCK)], axis=0
-            )
-            largest = jnp.max(stacked, axis=1, keepdims=True) + scale_epsilon
-            largest = jnp.broadcast_to(largest, stacked.shape)
-            scale = jnp.full(stacked.shape, 2.0**-23, F32)
-            inverse = jnp.full(stacked.shape, 2.0**23, F32)
-            for power in range(-23, 1):
-                above = largest > code_limit * 2.0**power
-                scale = jnp.where(above, 2.0 ** (power + 1), scale)
-                inverse = jnp.where(above, 2.0 ** -(power + 1), inverse)
+            value = base[:, here].astype(F32) + low_rank
+            by_column = jnp.max(jnp.abs(value), axis=0, keepdims=True)
+            views.append(here)
+            merged.append(value)
+            maxima += [by_column[:, start : start + BLOCK] for start in range(0, cw, BLOCK)]
+        stacked = jnp.concatenate(maxima, axis=0)
+        largest = jnp.max(stacked, axis=1, keepdims=True) + scale_epsilon
+        largest = jnp.broadcast_to(largest, stacked.shape)
+        scale = jnp.full(stacked.shape, 2.0**-23, F32)
+        inverse = jnp.full(stacked.shape, 2.0**23, F32)
+        for power in range(-23, 1):
+            above = largest > code_limit * 2.0**power
+            scale = jnp.where(above, 2.0 ** (power + 1), scale)
+            inverse = jnp.where(above, 2.0 ** -(power + 1), inverse)
+        for target in range(2 * NY):
             result = []
-            for index, start in enumerate(range(0, cw, BLOCK)):
-                codes = jnp.floor(
-                    merged[:, start : start + BLOCK] * inverse[index : index + 1] + 0.5
-                )
-                result.append((codes * scale[index : index + 1]).astype(BF16))
-            coded[:, here] = jnp.concatenate(result, axis=1)
+            for part in range(cw // BLOCK):
+                row = target * (cw // BLOCK) + part
+                block = merged[target][:, part * BLOCK : (part + 1) * BLOCK]
+                codes = jnp.floor(block * inverse[row : row + 1] + 0.5)
+                result.append((codes * scale[row : row + 1]).astype(BF16))
+            coded[:, views[target]] = jnp.concatenate(result, axis=1)
 
         for dy, dc in ((1, 0), (3, 0), (1, 1), (3, 1), (2, 0), (2, 1), (0, 1)):
             w_copy(q, ((y + dy) % NY) * 2 + (c + dc) % 2, t).start()
@@ -346,7 +350,9 @@
     stage_a(3), stage_a(4), stage_h(1), stage_h(2), stage_b(0)
     stage_a(5), stage_a(6), stage_h(3), stage_h(4), stage_b(1), stage_b(2)
     stage_a(7), stage_h(5), stage_h(6), stage_b(3), stage_b(4)
-    stage_h(7), stage_b(5), stage_b(6)
+    stage_h(7)
+    w_start(2), w_start(3)
+    stage_b(5), stage_b(6)
 
     def at_chunk(start, run):
         @pl.when((start >= 0) & (start % STRIDE == 0) & (start < STRIDE * CHUNKS))
@@ -360,13 +366,9 @@
             at_chunk(r - s - 1, functools.partial(ring_step, 0, s=s))
             at_chunk(r - s - 2, functools.partial(ring_step, 1, s=s))
 
-        @pl.when(r == 0)
+        @pl.when(r + 4 < CHUNKS)
         def _():
-            stage_b(7)
-
-        @pl.when(r + 2 < CHUNKS)
-        def _():
-            w_start(r + 2)
+            w_start(r + 4)
 
         for s in range(LAST + 1):
 
@@ -385,6 +387,10 @@
         at_chunk(r, arrive)
         for s in range(LAST, -1, -1):
             at_chunk(r - s, functools.partial(products, s=s))
+
+        @pl.when(r == 0)
+        def _():
+            stage_b(7)
 
     @pl.loop(1, groups)
     def _(step):
@@ -450,7 +456,7 @@
             *pair(CHUNKS),
         ],
         compiler_params=pltpu.CompilerParams(
-            collective_id=0, has_side_effects=True, vmem_limit_bytes=60 * 1024 * 1024
+            collective_id=0, has_side_effects=True, vmem_limit_bytes=50 * 1024 * 1024
         ),
     )(hidden, base, gain, down, up, cosine, sine)
 
@@ -461,7 +467,7 @@
     def shards(hidden, base_weight, adapter_down, adapter_up, norm_gain, positions):
         cosine, sine = frequencies(positions)
         return project(
-            hidden, base_weight, norm_gain[None, :], adapter_down.T, adapter_up,
+            hidden, base_weight, norm_gain.reshape(-1, 128), adapter_down.T, adapter_up,
             jnp.concatenate([cosine, cosine], axis=1),
             jnp.concatenate([-sine, sine], axis=1),
             groups, members,

time: 151 us -> 127 us (0.84)
  Pallas kernels: 146 us -> 121 us
    pallas_call x1, Pallas kernels: 146 us -> 121 us  [project(): pl.pallas_call(project_kernel, in_specs=[any_spec, any_spec] + [vmem_spec...]
    unnamed x1 -> x7, local copies, waits for them, and re-layouts: 1.88 us -> 3.47 us
where the time goes in v3:
time: 127 us; the launch traced here: 126 us
  Pallas kernels  121 us (95%)
  local copies, waits for them, and re-layouts  3.47 us (3%)
    pallas_call x1, Pallas kernels, project(): pl.pallas_call(project_kernel, in_specs=[any_spec, any_spec] + [vmem_spec...  121 us
    unnamed x7, local copies, waits for them, and re-layouts  3.47 us

profile of v3, /device:TPU:6, one launch (start us, length us, event | category | flops | bytes accessed | tf_op | source)
XLA Modules:
  0.0 126.0 jit_solution(3866963447715021)
XLA Ops:
  0.0 0.7 convert_element_type.3
  0.7 0.3 fusion
  1.0 0.1 pad_maximum_fusion
  1.1 0.0 copy-start
  1.1 1.2 copy-done
  2.3 0.0 copy-start.1
  2.3 0.8 copy-done.1
  3.1 0.0 copy-start.2
  3.1 0.7 copy-done.2
  3.8 121.4 %shard_map.64 = bf16[128,2048]{1,0:T(8,128)(2,1)S(1)} custom-call(bf16[128,16384]{1,0:T(8,128)(2,1)} %hidden_hbm.1, bf16[128,16384]{1,0:T(8,128)(2,1)} %base_hbm.1, bf16[128,128]{1,0:T(8,128)(2,1)S(1)} %bitcast.2, bf16[32,128]{1,0:T(8,128)(2,1)S(1)} %bitcast.3, bf16[32,16384]{1,0:T(8,128)(2,1)S(1)} %copy-done, f32[128,128]{1,0:T(8,128)S(1)} %get-tuple-element.8.cos_ref, ...), custom_call_target="tpu_custom_call" | custom-call | tf_op jit(solution)/shard_map/pallas_call | solution.py:429
  125.2 0.8 copy.8
  (1 shorter events, 0.0 us)
Async XLA Ops:
  1.1 1.2 copy-start
  2.3 0.8 copy-start.1
  3.1 0.7 copy-start.2

commit v4 on v3

--- a/solution.py
+++ b/solution.py
@@ -29,6 +29,7 @@
 STRIDE = 1
 LAST = NZ // 2
 OFFSETS = (4, 3, -3, 2, -2, 1, -1, 0)
+FAR = 5
 STEP_BLOCKS = ((0,), (1, 2), (3, 4), (5, 6), (7,))
 
 
@@ -49,7 +50,7 @@
 
 def project_kernel(
     hidden_hbm, base_hbm, gain_ref, down_ref, up_ref, cos_ref, sin_ref, out_ref,
-    hidden, base, normed, coded, acts, weights, sums, ring_z, ring_x, swap_x, swap_z,
+    hidden, base, normed, near, coded, acts, weights, sums, ring_z, ring_x, swap_x, swap_z,
     load_sem, local_sem, n_send, n_recv, a_send, a_recv, h_send, h_recv, b_send, b_recv,
     w_send, w_recv, rz_send, rz_recv, rx_send, rx_recv, sx_send, sx_recv, sz_send, sz_recv,
 ):
@@ -65,10 +66,16 @@
     groups = 2 * NZ
     width = hidden.shape[1]
 
-    load_hidden = pltpu.make_async_copy(hidden_hbm, hidden, load_sem.at[0])
-    load_base = pltpu.make_async_copy(base_hbm, base, load_sem.at[1])
-    load_hidden.start()
-    load_base.start()
+    parts = 4
+    part_width = width // parts
+
+    def load_hidden(part):
+        view = pl.ds(part * part_width, part_width)
+        return pltpu.make_async_copy(hidden_hbm.at[:, view], hidden.at[:, view], load_sem.at[part])
+
+    load_base = pltpu.make_async_copy(base_hbm, base, load_sem.at[parts])
+    for part in range(parts):
+        load_hidden(part).start()
 
     def zmod(value):
         return (value + NZ) % NZ
@@ -98,7 +105,6 @@
             device_id_type=pl.DeviceIdType.MESH,
         )
 
-    load_hidden.wait()
     span = width // groups
 
     def squares(group, total):
@@ -108,18 +114,28 @@
             total = total + part * part
         return total
 
-    total = lax.fori_loop(0, groups, squares, jnp.zeros((128, 128), F32))
+    total = jnp.zeros((128, 128), F32)
+    for part in range(parts):
+        load_hidden(part).wait()
+        if part == parts - 1:
+            load_base.start()
+        total = lax.fori_loop(
+            part * (groups // parts), (part + 1) * (groups // parts), squares, total
+        )
     mean_square = jnp.sum(total, axis=1, keepdims=True) / width
     members = 2 * NY
-    chosen = lax.broadcasted_iota(jnp.int32, (members, 128), 0) == t
     factor = jnp.broadcast_to(lax.rsqrt(mean_square + norm_epsilon), (128, 128))
+    row_index = lax.broadcasted_iota(jnp.int32, (members, 128), 0)
+
+    def normalized(group, member):
+        gains = gain_ref[lane(group, members), :].astype(F32)
+        gain = jnp.sum(jnp.where(row_index == member, gains, 0.0), axis=0, keepdims=True)
+        values = hidden[:, lane(group * members + member, 128)].astype(F32)
+        return (values * factor * gain).astype(BF16)
 
     @pl.loop(0, groups)
     def _(group):
-        mine = lane(group * members + t, 128)
-        gains = gain_ref[lane(group, members), :].astype(F32)
-        gain = jnp.sum(jnp.where(chosen, gains, 0.0), axis=0, keepdims=True)
-        normed[lane(group, 128), :] = (hidden[:, mine].astype(F32) * factor * gain).astype(BF16)
+        normed[lane(group, 128), :] = normalized(group, t)
 
     pl.semaphore_wait(barrier, groups - 1 + 2 * NY - 1)
 
@@ -129,14 +145,29 @@
             n_send.at[target], n_recv.at[source], {"fsdp": target},
         )
 
-    own_n = pltpu.make_async_copy(
-        normed.at[lane(f, 128), :], acts.at[lane(f, 128), lane(place, 128)], local_sem.at[0]
-    )
-    for offset in OFFSETS[:-1]:
-        for flip in (0, 1):
-            n_copy(f, zmod(z - offset) * 2 + (x + flip) % 2).start()
-    n_copy(f, z * 2 + 1 - x).start()
-    own_n.start()
+    def near_copy(n, source, target):
+        return remote(
+            near.at[n], acts.at[lane(source, 128), lane(c, 128 * NY)],
+            n_send.at[target], n_recv.at[source], {"fsdp": target},
+        )
+
+    def far_targets():
+        return [zmod(z - off) * 2 + (x + flip) % 2 for off in OFFSETS[:FAR] for flip in (0, 1)]
+
+    def near_targets():
+        ends = [(1, 0), (1, 1), (-1, 0), (-1, 1), (0, 1)]
+        return [zmod(z + dz) * 2 + (x + flip) % 2 for dz, flip in ends]
+
+    for target in far_targets():
+        n_copy(f, target).start()
+
+    def near_start():
+        for n, target in enumerate(near_targets()):
+            near[n] = jnp.concatenate([normalized(target, 2 * k + c) for k in range(NY)], axis=1)
+            near_copy(n, f, target).start()
+        for member in range(members):
+            column = ((member % 2) * NY + member // 2) * 128
+            acts[lane(f, 128), column : column + 128] = normalized(f, member)
 
     def w_copy(q, target, source):
         row = (source % 2) * NY + source // 2
@@ -202,19 +233,17 @@
         return remote(view, view, h_send.at[i, way], h_recv.at[i, way], {"tp": target * 2 + c})
 
     def b_copy(i, half):
-        view = acts.at[rows_of(i), lane(half, 128 * NY)]
+        rows = rows_of(i)
+        if i == NZ - 1:
+            rows = pl.ds(pl.multiple_of(z * 256 + (1 - x) * 128, 128), 128)
+        view = acts.at[rows, lane(half, 128 * NY)]
         return remote(view, view, b_send.at[i], b_recv.at[i], {"tp": y * 2 + 1 - c})
 
     down_y, up_y, far_y = (y + NY - 1) % NY, (y + 1) % NY, (y + 2) % NY
 
     def stage_a(i):
-        block = zmod(z + OFFSETS[i])
-        if OFFSETS[i]:
-            for other in (0, 1):
-                n_copy(block * 2 + other, f).wait_recv()
-        else:
-            n_copy(z * 2 + 1 - x, f).wait_recv()
-            own_n.wait()
+        for other in (0, 1):
+            n_copy(zmod(z + OFFSETS[i]) * 2 + other, f).wait_recv()
         for way in (0, 1):
             a_copy(i, y, way).start()
 
@@ -224,8 +253,14 @@
             h_copy(i, source, way).start()
 
     def stage_b(i):
-        for way in (0, 1):
-            h_copy(i, far_y, way).wait_recv()
+        if i < FAR:
+            for way in (0, 1):
+                h_copy(i, far_y, way).wait_recv()
+        elif OFFSETS[i]:
+            for other in (0, 1):
+                near_copy(0, zmod(z + OFFSETS[i]) * 2 + other, f).wait_recv()
+        else:
+            near_copy(0, z * 2 + 1 - x, f).wait_recv()
         b_copy(i, c).start()
 
     def stage_c(i):
@@ -288,13 +323,13 @@
 
         def read(start, count):
             rows = pl.ds(pl.multiple_of(start, count), count)
-            return sums[rows, here].astype(F32)
+            return sums[rows, here]
 
         def put(start, count, value):
             sums[pl.ds(pl.multiple_of(start, count), count), here] = value.astype(BF16)
 
         def swapped(i, start=0, count=size):
-            return swap_x[q, i, start : start + count].astype(F32)
+            return swap_x[q, i, start : start + count]
 
         if kind == 1:
             for i in STEP_BLOCKS[s]:
@@ -310,23 +345,23 @@
                 i = STEP_BLOCKS[s][way]
                 hop(s - 1).wait_recv()
                 if s == 1:
-                    near = first + way * half
-                    value = read(near, half) + slots[q, way, 0, 0:half].astype(F32)
+                    middle = first + way * half
+                    value = read(middle, half) + slots[q, way, 0, 0:half]
                     if kind == 1:
                         value = value + swapped(i, way * half, half)
                         other = first + (1 - way) * half
                         put(other, half, read(other, half) + swapped(i, (1 - way) * half, half))
-                    put(near, half, value)
+                    put(middle, half, value)
                 else:
-                    value = read(first, size) + slots[q, way, s - 1].astype(F32)
+                    value = read(first, size) + slots[q, way, s - 1]
                     if kind == 1:
                         value = value + swapped(i)
                     put(first, size, value)
                 hop(s).start()
         else:
-            value = read(first, size)
+            value = read(first, size).astype(F32)
             if kind == 1:
-                value = value + swapped(7)
+                value = value + swapped(7).astype(F32)
             for way in (0, 1):
                 ring(kind, q, s, way)[4](s - 1).wait_recv()
                 value = value + slots[q, way, s - 1].astype(F32)
@@ -344,20 +379,26 @@
 
     load_base.wait()
     w_start(0)
+    near_start()
     stage_a(0)
     w_start(1)
     stage_a(1), stage_a(2), stage_h(0)
     stage_a(3), stage_a(4), stage_h(1), stage_h(2), stage_b(0)
-    stage_a(5), stage_a(6), stage_h(3), stage_h(4), stage_b(1), stage_b(2)
-    stage_a(7), stage_h(5), stage_h(6), stage_b(3), stage_b(4)
-    stage_h(7)
+    stage_h(3), stage_h(4), stage_b(1), stage_b(2)
     w_start(2), w_start(3)
-    stage_b(5), stage_b(6)
+    stage_b(3), stage_b(4)
 
     def at_chunk(start, run):
         @pl.when((start >= 0) & (start % STRIDE == 0) & (start < STRIDE * CHUNKS))
         def _():
             run(start // STRIDE)
+
+    def arrive(q):
+        w_own(q).wait()
+
+        @pl.loop(1, 2 * NY)
+        def _(step):
+            w_copy(q, t, (t + step) % (2 * NY)).wait_recv()
 
     @pl.loop(0, STRIDE * (CHUNKS - 1) + LAST + 3)
     def _(r):
@@ -366,40 +407,32 @@
             at_chunk(r - s - 1, functools.partial(ring_step, 0, s=s))
             at_chunk(r - s - 2, functools.partial(ring_step, 1, s=s))
 
-        @pl.when(r + 4 < CHUNKS)
-        def _():
-            w_start(r + 4)
-
-        for s in range(LAST + 1):
-
             @pl.when(r == s)
             def _():
                 for i in STEP_BLOCKS[s]:
                     stage_c(i)
 
-        def arrive(q):
-            w_own(q).wait()
-
-            @pl.loop(1, 2 * NY)
-            def _(step):
-                w_copy(q, t, (t + step) % (2 * NY)).wait_recv()
-
-        at_chunk(r, arrive)
-        for s in range(LAST, -1, -1):
+            if s == 0:
+                at_chunk(r, arrive)
             at_chunk(r - s, functools.partial(products, s=s))
 
-        @pl.when(r == 0)
+        @pl.when(r == 1)
         def _():
-            stage_b(7)
-
-    @pl.loop(1, groups)
-    def _(step):
-        n_copy(f, (f + step) % groups).wait_send()
-
+            stage_b(5), stage_b(6), stage_b(7)
+
+        @pl.when(r + 4 < CHUNKS)
+        def _():
+            w_start(r + 4)
+
+    for target in far_targets():
+        n_copy(f, target).wait_send()
+    for n, target in enumerate(near_targets()):
+        near_copy(n, f, target).wait_send()
     for i in range(NZ):
-        for way in (0, 1):
-            a_copy(i, y, way).wait_send()
-            h_copy(i, y, way).wait_send()
+        if i < FAR:
+            for way in (0, 1):
+                a_copy(i, y, way).wait_send()
+                h_copy(i, y, way).wait_send()
         b_copy(i, c).wait_send()
 
     @pl.loop(0, CHUNKS)
@@ -435,6 +468,7 @@
             pltpu.VMEM((128, width), BF16),
             pltpu.VMEM((128, width), BF16),
             pltpu.VMEM((tokens, 128), BF16),
+            pltpu.VMEM((NZ - 3, 128, 128 * NY), BF16),
             pltpu.VMEM((128, width), BF16),
             pltpu.VMEM((tokens, members * BLOCK), BF16),
             pltpu.VMEM((members * BLOCK, cols), BF16),
@@ -443,7 +477,7 @@
             pltpu.VMEM((CHUNKS, 2, LAST, 128, tile), BF16),
             pltpu.VMEM((CHUNKS, NZ, 128, tile), BF16),
             pltpu.VMEM((CHUNKS, 128, tile), BF16),
-            dma((2,)),
+            dma((5,)),
             dma((1 + CHUNKS,)),
             *pair(groups),
             *pair(NZ, 2),
@@ -456,7 +490,7 @@
             *pair(CHUNKS),
         ],
         compiler_params=pltpu.CompilerParams(
-            collective_id=0, has_side_effects=True, vmem_limit_bytes=50 * 1024 * 1024
+            collective_id=0, has_side_effects=True, vmem_limit_bytes=56 * 1024 * 1024
         ),
     )(hidden, base, gain, down, up, cosine, sine)
 

time: 127 us -> 121 us (0.953)
  Pallas kernels: 121 us -> 117 us
  local copies, waits for them, and re-layouts: 3.47 us -> 1.88 us
    pallas_call x1, Pallas kernels: 121 us -> 117 us  [project(): pl.pallas_call(project_kernel, in_specs=[any_spec, any_spec] + [vmem_spec...]
    unnamed x7 -> x1, local copies, waits for them, and re-layouts: 3.47 us -> 1.88 us
where the time goes in v4:
time: 121 us
  Pallas kernels  117 us (97%)
  local copies, waits for them, and re-layouts  1.88 us (2%)
  other arithmetic  1.74 us (1%)
    pallas_call x1, Pallas kernels, project(): pl.pallas_call(project_kernel, in_specs=[any_spec, any_spec] + [vmem_spec...  117 us

profile of v4, /device:TPU:6, one launch (start us, length us, event | category | flops | bytes accessed | tf_op | source)
XLA Modules:
  0.0 120.7 jit_solution(1072217702476102938)
XLA Ops:
  0.0 0.7 convert_element_type.3
  0.7 0.3 fusion
  1.0 0.7 pad_maximum_fusion
  1.7 117.0 %shard_map.64 = bf16[128,2048]{1,0:T(8,128)(2,1)} custom-call(bf16[128,16384]{1,0:T(8,128)(2,1)} %hidden_hbm.1, bf16[128,16384]{1,0:T(8,128)(2,1)} %base_hbm.1, bf16[128,128]{1,0:T(8,128)(2,1)} %bitcast.2, bf16[32,128]{1,0:T(8,128)(2,1)} %bitcast.3, bf16[32,16384]{1,0:T(8,128)(2,1)} %up_ref.1, f32[128,128]{1,0:T(8,128)} %get-tuple-element.8.cos_ref, ...), custom_call_target="tpu_custom_call" | custom-call | tf_op jit(solution)/shard_map/pallas_call | solution.py:462
  118.8 1.9 %copy.8 = bf16[128,2048]{1,0:T(8,128)(2,1)} copy(bf16[128,2048]{1,0:T(8,128)(2,1)} %shard_map.64) | data formatting | bytes 1048576
  (1 shorter events, 0.0 us)
